TPU v7x, 512 devices: a whole 4x4x16 slice. The times are simulated.
512 devices in a mesh: filter: 32 (over z_lo, x), space: 16 (over z_hi, y, core).
Axes of the slice: x: 4, y: 4, z: 16 (z_hi: 2, z_lo: 8; z = z_hi * 8 + z_lo), core: 2. Of those that a mesh axis runs over, the one named last changes fastest.
Arguments:
- volume: bfloat16 [1024, 64, 1024], P('filter', 'space'), may hold values from -6 to 6
- mixing: bfloat16 [1024, 1024], P('filter'), may hold values from -0.1875 to 0.1875
- kernel_taps: float32 [1024, 27], P('filter'), may hold values from -1.25 to 1.25
- upstream: bfloat16 [1024, 64, 1024], P('filter', 'space'), may hold values from -6 to 6
Outputs:
- output: bfloat16 [1024, 64, 1024], P('filter', 'space')
- volume_grad: bfloat16 [1024, 64, 1024], P('filter', 'space')
- mixing_grad: float32 [1024, 1024], P('filter', 'space')
- taps_grad: float32 [1024, 27], P('filter')
All inputs are finite; a program needn't handle non-finite values.
Results may differ from a plain program's by a relative error of at most 0.0055.
Values may be sent and summed in bfloat16 or wider, within the bound.
A program may use at most 64 MiB of HBM per device.

v0:
```python
import math
import jax
import jax.numpy as jnp
from jax import lax
from jax.sharding import PartitionSpec as P

WW = 64


def padded_2(array, sides, width):
    for axis, dim in sides:
        size, length = (lax.axis_size(axis), array.shape[dim])
        up = [(i, (i + 1) % size) for i in range(size - 1)]
        down = [(j, i) for i, j in up]
        last = lax.slice_in_dim(array, length - width, length, axis=dim)
        leading = lax.slice_in_dim(array, 0, width, axis=dim)
        before = lax.ppermute(last, axis, up)
        after = lax.ppermute(leading, axis, down)
        array = jnp.concatenate([before, array, after], axis=dim)
    return array


def pad_rows_cols(field):
    return jnp.pad(field, ((0, 0), (0, 0), (1, 1), (1, 1)))


def depth_conv(padded, kernel_taps, flip):
    depth = padded.shape[1] - 2
    height = padded.shape[2] - 2
    breadth = padded.shape[3] - 2
    summed = jnp.zeros((padded.shape[0], depth, height, breadth), jnp.float32)
    for plane_off in range(3):
        for row_off in range(3):
            for col_off in range(3):
                index_tap = plane_off * 9 + row_off * 3 + col_off
                if flip:
                    plane_at, row_at, col_at = (2 - plane_off, 2 - row_off, 2 - col_off)
                else:
                    plane_at, row_at, col_at = (plane_off, row_off, col_off)
                window = padded[
                    :,
                    plane_at : plane_at + depth,
                    row_at : row_at + height,
                    col_at : col_at + breadth,
                ]
                summed = summed + kernel_taps[:, index_tap][:, None, None, None] * window.astype(
                    jnp.float32
                )
    return summed


def tap_grads(grad_field, padded):
    depth = grad_field.shape[1]
    height = grad_field.shape[2]
    breadth = grad_field.shape[3]
    grad_wide = grad_field.astype(jnp.float32)
    columns_list = []
    for plane_off in range(3):
        for row_off in range(3):
            for col_off in range(3):
                window = padded[
                    :,
                    plane_off : plane_off + depth,
                    row_off : row_off + height,
                    col_off : col_off + breadth,
                ]
                columns_list.append(jnp.sum(grad_wide * window.astype(jnp.float32), axis=(1, 2, 3)))
    return jnp.stack(columns_list, axis=1)


def silu_slope(values):
    sig_val = jax.nn.sigmoid(values)
    return sig_val * (1.0 + values * (1.0 - sig_val))


def body(volume, mixing, kernel_taps, upstream):
    channels = volume.shape[0]
    planes = volume.shape[1]
    flat_cells = volume.shape[2]
    row_count = flat_cells // WW
    slab_cells = planes * flat_cells
    space_count = lax.axis_size("space")
    norm_factor = 1.0 / math.sqrt(planes * space_count * flat_cells)
    flat_vol = volume.reshape(channels, slab_cells)
    vol_all = lax.all_gather(flat_vol, "filter", axis=0, tiled=True)
    mixed = jnp.dot(mixing, vol_all, preferred_element_type=jnp.float32).astype(jnp.bfloat16)
    mixed_grid = mixed.reshape(channels, planes, row_count, WW)
    up_grid = upstream.reshape(channels, planes, row_count, WW)
    mixed_rim = padded_2(mixed_grid, (("space", 1),), 1)
    mixed_pad = pad_rows_cols(mixed_rim)
    spatial = depth_conv(mixed_pad, kernel_taps, False)
    grad_own = (up_grid.astype(jnp.float32) * silu_slope(spatial)).astype(jnp.bfloat16)
    grad_wide = padded_2(grad_own, (("space", 1),), 1)
    vol_grid = volume.reshape(channels, planes, row_count, WW).astype(jnp.float32)
    output = (
        (vol_grid + jax.nn.silu(spatial)).astype(jnp.bfloat16).reshape(channels, planes, flat_cells)
    )
    spatial_grad = grad_wide[:, 1:-1]
    mixed_grad = (
        depth_conv(pad_rows_cols(grad_wide), kernel_taps, True)
        .astype(jnp.bfloat16)
        .reshape(channels, slab_cells)
    )
    taps_part = tap_grads(spatial_grad, mixed_pad) * norm_factor
    taps_grad = lax.psum(taps_part, "space")
    weight_cols = lax.all_to_all(mixing, "filter", split_axis=1, concat_axis=0, tiled=True)
    back_sum = lax.dot_general(
        weight_cols,
        lax.all_gather(mixed_grad, "filter", axis=0, tiled=True),
        (((0,), (0,)), ((), ())),
        preferred_element_type=jnp.float32,
    )
    weight_term = (
        lax.dot_general(
            mixed_grad, vol_all, (((1,), (1,)), ((), ())), preferred_element_type=jnp.float32
        )
        * norm_factor
    )
    mixing_grad = lax.psum_scatter(weight_term, "space", scatter_dimension=1, tiled=True)
    volume_grad = (
        (upstream.reshape(channels, slab_cells).astype(jnp.float32) + back_sum)
        .astype(jnp.bfloat16)
        .reshape(channels, planes, flat_cells)
    )
    return (output, volume_grad, mixing_grad, taps_grad)


def solution(mesh):
    in_specs = (
        P("filter", "space", None),
        P("filter", None),
        P("filter", None),
        P("filter", "space", None),
    )
    out_specs = (
        P("filter", "space", None),
        P("filter", "space", None),
        P("filter", "space"),
        P("filter", None),
    )
    return jax.shard_map(body, mesh=mesh, in_specs=in_specs, out_specs=out_specs, check_vma=False)
```

profile of v0, /device:TPU:2, one launch (start us, length us, event | category | flops | bytes accessed | tf_op | source)
XLA Modules:
  0.0 667.5 jit_solution(4207602100597087472)
XLA Ops:
  7.2 1.7 copy.16
  9.0 1.3 reshape.69
  10.3 2.0 slice_reduce_fusion.26
  12.3 240.9 %all-gather.3.cloned.1.call-done = bf16[1024,4096]{1,0:T(8,128)(2,1)} async-done(((bf16[32,4096]{1,0:T(8,128)(2,1)}), bf16[1024,4096]{1,0:T(8,128)(2,1)}) %all-gather.3.cloned.1.call-update) | async-done | bytes 8388624 | tf_op jit(solution)/shard_map/all_gather | solution.py:85
  253.2 4.9 convolution_convert_fusion
  258.7 1.3 collective-permute-start
  260.0 1.3 collective-permute-start.1
  261.7 2.8 collective-permute-done.1
  265.3 11.5 %fusion.72 = (f32[32]{0:T(128)S(1)}, f32[32]{0:T(128)S(1)}, f32[32]{0:T(128)S(1)}, f32[32]{0:T(128)S(1)}, f32[32]{0:T(128)}, /*index=5*/f32[32]{0:T(128)}, f32[3...) fusion(bf16[32,6,18,66]{3,2,1,0:T(8,128)(2,1)S(1)} %select_maxi, ...), kind=kLoop, calls=%fused_computation.138 | loop fusion | flops 16776640 | bytes 8001152 | tf_op jit(solution)/shard_map/reduce_sum | solution.py:67
  276.8 5.5 collective-permute-start.2
  282.3 1.3 collective-permute-start.3
  283.6 1.9 collective-permute-done.3
  286.3 5.8 fusion.73
  292.6 6.1 convolution_multiply_fusion
  301.6 12.2 %all-to-all-start = ((bf16[32,2,512]{2,1,0:T(2,128)(2,1)}), bf16[32,2,512]{2,1,0:T(2,128)(2,1)}, u32[]{:S(2)}, u32[]{:S(2)}) async-start(bf16[32,2,512]{2,1,0:T(2,128)(2,1)} %reshape.99), calls=%async_computation | async-start | bytes 131072 | tf_op jit(solution)/shard_map/all_to_all | solution.py:106
  313.9 1.3 reshape.67
  316.3 9.2 %all-to-all-done = bf16[32,2,512]{2,1,0:T(2,128)(2,1)} async-done(((bf16[32,2,512]{2,1,0:T(2,128)(2,1)}), bf16[32,2,512]{2,1,0:T(2,128)(2,1)}, u32[]{:S(2)}, u32[]{:S(2)}) %all-to-all-start) | async-done | bytes 65568 | tf_op jit(solution)/shard_map/all_to_all | solution.py:106
  327.6 3.0 fusion.71
  330.6 2.9 stack.111
  333.5 126.2 %psum.7 = f32[32,27]{0,1:T(8,128)S(1)} all-reduce(f32[32,27]{0,1:T(8,128)S(1)} %broadcast_multiply_fusion), channel_id=1, replica_groups=mesh['filter'=32,'space'=16] {'space'}, use_global_device_ids=true, to_apply=%region_28.29 | all-reduce | flops 864 | bytes 6912 | tf_op jit(solution)/shard_map/psum | solution.py:105
  460.3 1.5 add_convert_fusion
  462.8 1.4 copy.15
  464.3 190.9 %all-gather.5.cloned.1.call-done = bf16[1024,4096]{1,0:T(8,128)(2,1)} async-done(((bf16[32,4096]{1,0:T(8,128)(2,1)}), bf16[1024,4096]{1,0:T(8,128)(2,1)}) %all-gather.5.cloned.1.call-update) | async-done | bytes 8388624 | tf_op jit(solution)/shard_map/all_gather | solution.py:109
  655.2 4.9 fusion.1
  (55 shorter events, 11.7 us)
Async XLA Ops:
  7.2 246.1 %copy-start.11 = (bf16[32,1024]{1,0:T(8,128)(2,1)S(1)}, bf16[32,1024]{1,0:T(8,128)(2,1)}, u32[]{:S(2)}) copy-start(bf16[32,1024]{1,0:T(8,128)(2,1)} %param.5) | copy-start | bytes 196612
  7.2 246.0 %all-gather.3.cloned.1.call-start = ((), (), s32[]{:S(2)}) async-start(), calls=%async_computation.2 | async-start | bytes 8650752 | tf_op jit(solution)/shard_map/all_gather | solution.py:85
  9.0 453.8 %reduce-scatter.4.cloned.1.call-start = ((), (), s32[]{:S(2)}) async-start(), calls=%async_computation.4 | async-start | bytes 557056
  12.3 249.0 %copy-start = (f32[32,27]{1,0:T(8,128)S(1)}, f32[32,27]{1,0:T(8,128)}, u32[]{:S(2)}) copy-start(f32[32,27]{1,0:T(8,128)} %param.6) | copy-start | bytes 10372
  258.7 2.9 collective-permute-start
  260.0 4.5 collective-permute-start.1
  261.7 15.1 %copy-start.4 = (bf16[32,1,16,64]{3,2,1,0:T(8,128)(2,1)}, bf16[32,1,16,64]{3,2,1,0:T(8,128)(2,1)S(1)}, u32[]{:S(2)}) copy-start(bf16[32,1,16,64]{3,2,1,0:T(8,128)(2,1)S(1)} %collective-permute-done) | copy-start | bytes 196612
  264.5 12.3 %copy-start.6 = (bf16[32,1,16,64]{3,2,1,0:T(8,128)(2,1)}, bf16[32,1,16,64]{3,2,1,0:T(8,128)(2,1)S(1)}, u32[]{:S(2)}) copy-start(bf16[32,1,16,64]{3,2,1,0:T(8,128)(2,1)S(1)} %collective-permute-done.1) | copy-start | bytes 196612
  276.8 6.8 %collective-permute-start.2 = (bf16[32,1,16,64]{3,2,1,0:T(8,128)(2,1)S(1)}, bf16[32,1,16,64]{3,2,1,0:T(8,128)(2,1)S(1)}, u32[]{:S(2)}, u32[]{:S(2)}) collective-permute-start(bf16[32,1,16,64]{3,2,1,0:T(8,128)(2,1)S(1)} %get-tuple-element.75), channel_id=1, source_target_pairs={{0,1},{1,2},{2,3},{3,4},{4,5},{5,6},{6,7},{7,8},{8,9},{9,10},{10,1... | collective-permute-start | bytes 196616 | tf_op jit(solution)/shard_map/ppermute | solution.py:17
  282.3 3.2 collective-permute-start.3
  292.6 6.1 copy-start.2
  292.6 7.9 %copy-start.12 = (bf16[32,1024]{1,0:T(8,128)(2,1)S(1)}, bf16[32,1024]{1,0:T(8,128)(2,1)}, u32[]{:S(2)}) copy-start(bf16[32,1024]{1,0:T(8,128)(2,1)} %param.5) | copy-start | bytes 196612
  298.7 15.1 %copy-start.8 = (bf16[32,4,1024]{2,1,0:T(4,128)(2,1)S(1)}, bf16[32,4,1024]{2,1,0:T(4,128)(2,1)}, u32[]{:S(2)}) copy-start(bf16[32,4,1024]{2,1,0:T(4,128)(2,1)} %param.7) | copy-start | bytes 786436
  298.7 15.2 %copy-start.9 = (bf16[32,4,1024]{2,1,0:T(4,128)(2,1)S(1)}, bf16[32,4,1024]{2,1,0:T(4,128)(2,1)}, u32[]{:S(2)}) copy-start(bf16[32,4,1024]{2,1,0:T(4,128)(2,1)} %param.4) | copy-start | bytes 786436
  299.8 355.4 %all-gather.5.cloned.1.call-start = ((), (), s32[]{:S(2)}) async-start(), calls=%async_computation.3 | async-start | bytes 8650752 | tf_op jit(solution)/shard_map/all_gather | solution.py:109
  301.6 23.9 %all-to-all-start = ((bf16[32,2,512]{2,1,0:T(2,128)(2,1)}), bf16[32,2,512]{2,1,0:T(2,128)(2,1)}, u32[]{:S(2)}, u32[]{:S(2)}) async-start(bf16[32,2,512]{2,1,0:T(2,128)(2,1)} %reshape.99), calls=%async_computation | async-start | bytes 131072 | tf_op jit(solution)/shard_map/all_to_all | solution.py:106
  313.8 13.8 %copy-start.5 = (bf16[32,1,16,64]{3,2,1,0:T(8,128)(2,1)S(1)}, bf16[32,1,16,64]{3,2,1,0:T(8,128)(2,1)}, u32[]{:S(2)}) copy-start(bf16[32,1,16,64]{3,2,1,0:T(8,128)(2,1)} %copy-done.4) | copy-start | bytes 196612
  313.8 13.8 %copy-start.7 = (bf16[32,1,16,64]{3,2,1,0:T(8,128)(2,1)S(1)}, bf16[32,1,16,64]{3,2,1,0:T(8,128)(2,1)}, u32[]{:S(2)}) copy-start(bf16[32,1,16,64]{3,2,1,0:T(8,128)(2,1)} %copy-done.6) | copy-start | bytes 196612
  327.6 132.7 %copy-start.1 = (f32[32,4,16,64]{3,2,1,0:T(8,128)S(1)}, f32[32,4,16,64]{3,2,1,0:T(8,128)}, u32[]{:S(2)}) copy-start(f32[32,4,16,64]{3,2,1,0:T(8,128)} %get-tuple-element.74) | copy-start | bytes 1572868
  330.6 324.6 %copy-start.3 = (f32[4,8,4,1024]{3,1,2,0:T(8,128)S(1)}, f32[4,8,4,1024]{3,1,2,0:T(8,128)}, u32[]{:S(2)}) copy-start(f32[4,8,4,1024]{3,1,2,0:T(8,128)} %copy.17) | copy-start | bytes 1572868
  330.6 324.6 %copy-start.10 = (bf16[1024,32]{0,1:T(8,128)(2,1)S(1)}, bf16[1024,32]{0,1:T(8,128)(2,1)}, u32[]{:S(2)}) copy-start(bf16[1024,32]{0,1:T(8,128)(2,1)} %all_to_all.17) | copy-start | bytes 196612
Sparse Core Ops, SparseCore 0:
  10.7 242.5 all-gather.2
  299.9 123.4 reduce-scatter.3
  426.2 228.9 all-gather.4
where the time goes:
time: 668 us
  waiting for transfers between devices  447 us (67%)
  blocking collectives  126 us (19%)
  other arithmetic  23.4 us (4%)
  starting transfers between devices  21.7 us (3%)
  local copies, waits for them, and re-layouts  19.8 us (3%)
  matrix products  15.9 us (2%)
  between operations  14 us (2%)
    all_gather x1, waiting for transfers between devices, body(): vol_all = lax.all_gather(flat_vol, 'filter', axis=0, tiled=True)  241 us
    all_gather x1, waiting for transfers between devices, body(): lax.all_gather(mixed_grad, 'filter', axis=0, tiled=True)  191 us
    psum x1, blocking collectives, body(): taps_grad = lax.psum(taps_part, 'space')  126 us
    reduce_sum x2, other arithmetic, tap_grads(): jnp.sum(grad_wide * window.astype(jnp.float32), axis=(1, 2, 3))  14.4 us
  transfers between devices with their start and end apart: 8, of which 5 were waited for; matrix products, arithmetic and copies ran while one was open for 3% of the time, Pallas kernels for 0%

commit v1 on v0

--- a/solution.py
+++ b/solution.py
@@ -5,6 +5,15 @@
 from jax.sharding import PartitionSpec as P
 
 WW = 64
+
+
+def link_kinds(row_data, net_axis):
+    return jnp.concatenate(
+        lax.all_to_all(
+            jnp.stack([row_data for _ in range(lax.axis_size(net_axis))], 0), net_axis, 0, 0
+        ),
+        axis=0,
+    )
 
 
 def padded_2(array, sides, width):
@@ -106,7 +115,7 @@
     weight_cols = lax.all_to_all(mixing, "filter", split_axis=1, concat_axis=0, tiled=True)
     back_sum = lax.dot_general(
         weight_cols,
-        lax.all_gather(mixed_grad, "filter", axis=0, tiled=True),
+        link_kinds(mixed_grad, "filter"),
         (((0,), (0,)), ((), ())),
         preferred_element_type=jnp.float32,
     )

time: 668 us -> 822 us (1.23)
  the two profiles are of different devices: /device:TPU:2 before, /device:TPU:420 now
where the time goes in v1:
time: 822 us; the launch traced here: 821 us
  blocking collectives  445 us (54%)
  waiting for transfers between devices  205 us (25%)
  starting transfers between devices  86.4 us (11%)
  other arithmetic  27.4 us (3%)
  local copies, waits for them, and re-layouts  25.8 us (3%)
  matrix products  16.2 us (2%)
  between operations  15.1 us (2%)
    psum x1, blocking collectives, body(): taps_grad = lax.psum(taps_part, 'space')  445 us
    all_gather x1, waiting for transfers between devices, body(): vol_all = lax.all_gather(flat_vol, 'filter', axis=0, tiled=True)  203 us
    all_to_all x1, starting transfers between devices, body(): lax.all_to_all(mixing, 'filter', split_axis=1, concat_axis=0, tiled=True)  40.6 us
    ppermute x2, starting transfers between devices, padded_2(): after = lax.ppermute(leading, axis, down)  29.1 us
  transfers between devices with their start and end apart: 8, of which 3 were waited for; matrix products, arithmetic and copies ran while one was open for 5% of the time, Pallas kernels for 0%

profile of v1, /device:TPU:420, one launch (start us, length us, event | category | flops | bytes accessed | tf_op | source)
XLA Modules:
  0.0 820.8 jit_solution(9270872690832561117)
XLA Ops:
  7.2 1.7 copy.16
  10.2 2.5 slice_reduce_fusion.26
  13.0 203.2 %all-gather.2.cloned.1.call-done = bf16[1024,4096]{1,0:T(8,128)(2,1)} async-done(((bf16[32,4096]{1,0:T(8,128)(2,1)}), bf16[1024,4096]{1,0:T(8,128)(2,1)}) %all-gather.2.cloned.1.call-update) | async-done | bytes 8388624 | tf_op jit(solution)/shard_map/all_gather | solution.py:94
  216.2 4.9 convolution_convert_fusion
  221.7 1.9 collective-permute-start
  223.6 14.5 %collective-permute-start.1 = (bf16[32,1,16,64]{3,2,1,0:T(8,128)(2,1)S(1)}, bf16[32,1,16,64]{3,2,1,0:T(8,128)(2,1)S(1)}, u32[]{:S(2)}, u32[]{:S(2)}) collective-permute-start(bf16[32,1,16,64]{3,2,1,0:T(8,128)(2,1)S(1)} %get-tuple-element.78), channel_id=1, source_target_pairs={{1,0},{2,1},{3,2},{4,3},{5,4},{6,5},{7,6},{8,7},{9,8},{10,9},{11,1... | collective-permute-start | bytes 196616 | tf_op jit(solution)/shard_map/ppermute | solution.py:27
  238.8 1.8 collective-permute-done.1
  241.6 11.5 %fusion.72 = (f32[32]{0:T(128)}, f32[32]{0:T(128)}, f32[32]{0:T(128)}, f32[32]{0:T(128)}, f32[32]{0:T(128)}, /*index=5*/f32[32]{0:T(128)}, f32[32]{0:T(128)}, f3...) fusion(bf16[32,6,18,66]{3,2,1,0:T(8,128)(2,1)S(1)} %select_maxi, ...), kind=kLoop, calls=%fused_computation.138 | loop fusion | flops 16776640 | bytes 8001152 | tf_op jit(solution)/shard_map/reduce_sum | solution.py:76
  253.3 1.9 collective-permute-start.2
  255.2 14.6 %collective-permute-start.3 = (bf16[32,1,16,64]{3,2,1,0:T(8,128)(2,1)S(1)}, bf16[32,1,16,64]{3,2,1,0:T(8,128)(2,1)S(1)}, u32[]{:S(2)}, u32[]{:S(2)}) collective-permute-start(bf16[32,1,16,64]{3,2,1,0:T(8,128)(2,1)S(1)} %get-tuple-element.76), channel_id=1, source_target_pairs={{1,0},{2,1},{3,2},{4,3},{5,4},{6,5},{7,6},{8,7},{9,8},{10,9},{11,1... | collective-permute-start | bytes 196616 | tf_op jit(solution)/shard_map/ppermute | solution.py:27
  271.7 40.6 %all-to-all-start.1 = ((bf16[32,2,512]{2,1,0:T(2,128)(2,1)}), bf16[32,2,512]{2,1,0:T(2,128)(2,1)S(1)}, u32[]{:S(2)}, u32[]{:S(2)}) async-start(bf16[32,2,512]{2,1,0:T(2,128)(2,1)} %reshape.100), calls=%async_computation.1 | async-start | bytes 131072 | tf_op jit(solution)/shard_map/all_to_all | solution.py:115
  313.3 6.7 fusion.73
  320.5 4.3 stack.87
  324.8 12.6 %all-to-all-start = ((bf16[32,32,4096]{2,1,0:T(8,128)(2,1)}), bf16[32,32,4096]{2,1,0:T(8,128)(2,1)}, u32[]{:S(2)}, u32[]{:S(2)}) async-start(bf16[32,32,4096]{2,1,0:T(8,128)(2,1)} %stack.87), calls=%async_computation | async-start | bytes 16777216 | tf_op jit(solution)/shard_map/all_to_all | solution.py:12
  337.6 1.9 convert_element_type.292
  339.5 2.2 reshape.67
  341.7 2.2 copy.17
  343.9 1.8 reshape.101
  345.7 2.4 add_convert_fusion
  348.1 2.1 reshape.65
  350.3 3.4 fusion.71
  354.0 6.0 convolution_multiply_fusion
  361.1 444.6 %psum.7 = f32[32,27]{0,1:T(8,128)S(1)} all-reduce(f32[32,27]{0,1:T(8,128)S(1)} %broadcast_multiply_fusion), channel_id=1, replica_groups=mesh['filter'=32,'space'=16] {'space'}, use_global_device_ids=true, to_apply=%region_28.29 | all-reduce | flops 864 | bytes 6912 | tf_op jit(solution)/shard_map/psum | solution.py:114
  807.8 5.2 fusion.1
  (156 shorter events, 11.2 us)
Async XLA Ops:
  7.2 209.0 %all-gather.2.cloned.1.call-start = ((), (), s32[]{:S(2)}) async-start(), calls=%async_computation.3 | async-start | bytes 8650752 | tf_op jit(solution)/shard_map/all_gather | solution.py:94
  12.8 228.6 %copy-start.10 = (f32[32]{0:T(128)}, f32[32]{0:T(128)S(1)}, u32[]{:S(2)}) copy-start(f32[32]{0:T(128)S(1)} %get-tuple-element.51) | copy-start | bytes 388
  12.8 228.6 %copy-start.12 = (f32[32]{0:T(128)}, f32[32]{0:T(128)S(1)}, u32[]{:S(2)}) copy-start(f32[32]{0:T(128)S(1)} %get-tuple-element.52) | copy-start | bytes 388
  12.8 228.6 %copy-start.14 = (f32[32]{0:T(128)}, f32[32]{0:T(128)S(1)}, u32[]{:S(2)}) copy-start(f32[32]{0:T(128)S(1)} %get-tuple-element.53) | copy-start | bytes 388
  12.8 228.6 %copy-start.16 = (f32[32]{0:T(128)}, f32[32]{0:T(128)S(1)}, u32[]{:S(2)}) copy-start(f32[32]{0:T(128)S(1)} %get-tuple-element.54) | copy-start | bytes 388
  12.8 228.6 %copy-start.18 = (f32[32]{0:T(128)}, f32[32]{0:T(128)S(1)}, u32[]{:S(2)}) copy-start(f32[32]{0:T(128)S(1)} %get-tuple-element.55) | copy-start | bytes 388
  12.9 228.6 %copy-start.20 = (f32[32]{0:T(128)}, f32[32]{0:T(128)S(1)}, u32[]{:S(2)}) copy-start(f32[32]{0:T(128)S(1)} %get-tuple-element.56) | copy-start | bytes 388
  12.9 228.6 %copy-start.22 = (f32[32]{0:T(128)}, f32[32]{0:T(128)S(1)}, u32[]{:S(2)}) copy-start(f32[32]{0:T(128)S(1)} %get-tuple-element.57) | copy-start | bytes 388
  12.9 228.6 %copy-start.24 = (f32[32]{0:T(128)}, f32[32]{0:T(128)S(1)}, u32[]{:S(2)}) copy-start(f32[32]{0:T(128)S(1)} %get-tuple-element.58) | copy-start | bytes 388
  12.9 228.6 %copy-start.26 = (f32[32]{0:T(128)}, f32[32]{0:T(128)S(1)}, u32[]{:S(2)}) copy-start(f32[32]{0:T(128)S(1)} %get-tuple-element.59) | copy-start | bytes 388
  12.9 228.6 %copy-start.28 = (f32[32]{0:T(128)}, f32[32]{0:T(128)S(1)}, u32[]{:S(2)}) copy-start(f32[32]{0:T(128)S(1)} %get-tuple-element.60) | copy-start | bytes 388
  12.9 228.6 %copy-start.30 = (f32[32]{0:T(128)}, f32[32]{0:T(128)S(1)}, u32[]{:S(2)}) copy-start(f32[32]{0:T(128)S(1)} %get-tuple-element.61) | copy-start | bytes 388
  12.9 228.6 %copy-start.32 = (f32[32]{0:T(128)}, f32[32]{0:T(128)S(1)}, u32[]{:S(2)}) copy-start(f32[32]{0:T(128)S(1)} %get-tuple-element.62) | copy-start | bytes 388
  12.9 228.6 %copy-start.34 = (f32[32]{0:T(128)}, f32[32]{0:T(128)S(1)}, u32[]{:S(2)}) copy-start(f32[32]{0:T(128)S(1)} %get-tuple-element.63) | copy-start | bytes 388
  12.9 228.6 %copy-start.36 = (f32[32]{0:T(128)}, f32[32]{0:T(128)S(1)}, u32[]{:S(2)}) copy-start(f32[32]{0:T(128)S(1)} %get-tuple-element.64) | copy-start | bytes 388
  221.7 17.1 %collective-permute-start = (bf16[32,1,16,64]{3,2,1,0:T(8,128)(2,1)S(1)}, bf16[32,1,16,64]{3,2,1,0:T(8,128)(2,1)S(1)}, u32[]{:S(2)}, u32[]{:S(2)}) collective-permute-start(bf16[32,1,16,64]{3,2,1,0:T(8,128)(2,1)S(1)} %get-tuple-element.77), channel_id=1, source_target_pairs={{0,1},{1,2},{2,3},{3,4},{4,5},{5,6},{6,7},{7,8},{8,9},{9,10},{10,1... | collective-permute-start | bytes 196616 | tf_op jit(solution)/shard_map/ppermute | solution.py:26
  223.6 17.0 %collective-permute-start.1 = (bf16[32,1,16,64]{3,2,1,0:T(8,128)(2,1)S(1)}, bf16[32,1,16,64]{3,2,1,0:T(8,128)(2,1)S(1)}, u32[]{:S(2)}, u32[]{:S(2)}) collective-permute-start(bf16[32,1,16,64]{3,2,1,0:T(8,128)(2,1)S(1)} %get-tuple-element.78), channel_id=1, source_target_pairs={{1,0},{2,1},{3,2},{4,3},{5,4},{6,5},{7,6},{8,7},{9,8},{10,9},{11,1... | collective-permute-start | bytes 196616 | tf_op jit(solution)/shard_map/ppermute | solution.py:27
  253.3 59.0 %collective-permute-start.2 = (bf16[32,1,16,64]{3,2,1,0:T(8,128)(2,1)S(1)}, bf16[32,1,16,64]{3,2,1,0:T(8,128)(2,1)S(1)}, u32[]{:S(2)}, u32[]{:S(2)}) collective-permute-start(bf16[32,1,16,64]{3,2,1,0:T(8,128)(2,1)S(1)} %get-tuple-element.75), channel_id=1, source_target_pairs={{0,1},{1,2},{2,3},{3,4},{4,5},{5,6},{6,7},{7,8},{8,9},{9,10},{10,1... | collective-permute-start | bytes 196616 | tf_op jit(solution)/shard_map/ppermute | solution.py:26
  255.2 57.1 %collective-permute-start.3 = (bf16[32,1,16,64]{3,2,1,0:T(8,128)(2,1)S(1)}, bf16[32,1,16,64]{3,2,1,0:T(8,128)(2,1)S(1)}, u32[]{:S(2)}, u32[]{:S(2)}) collective-permute-start(bf16[32,1,16,64]{3,2,1,0:T(8,128)(2,1)S(1)} %get-tuple-element.76), channel_id=1, source_target_pairs={{1,0},{2,1},{3,2},{4,3},{5,4},{6,5},{7,6},{8,7},{9,8},{10,9},{11,1... | collective-permute-start | bytes 196616 | tf_op jit(solution)/shard_map/ppermute | solution.py:27
  271.7 48.7 %all-to-all-start.1 = ((bf16[32,2,512]{2,1,0:T(2,128)(2,1)}), bf16[32,2,512]{2,1,0:T(2,128)(2,1)S(1)}, u32[]{:S(2)}, u32[]{:S(2)}) async-start(bf16[32,2,512]{2,1,0:T(2,128)(2,1)} %reshape.100), calls=%async_computation.1 | async-start | bytes 131072 | tf_op jit(solution)/shard_map/all_to_all | solution.py:115
  324.8 483.1 %all-to-all-start = ((bf16[32,32,4096]{2,1,0:T(8,128)(2,1)}), bf16[32,32,4096]{2,1,0:T(8,128)(2,1)}, u32[]{:S(2)}, u32[]{:S(2)}) async-start(bf16[32,32,4096]{2,1,0:T(8,128)(2,1)} %stack.87), calls=%async_computation | async-start | bytes 16777216 | tf_op jit(solution)/shard_map/all_to_all | solution.py:12
  337.4 469.0 %reduce-scatter.4.cloned.1.call-start = ((), (), s32[]{:S(2)}) async-start(), calls=%async_computation.4 | async-start | bytes 557056
  354.0 453.9 %copy-start.2 = (f32[4,8,4,1024]{3,1,2,0:T(8,128)S(1)}, f32[4,8,4,1024]{3,1,2,0:T(8,128)}, u32[]{:S(2)}) copy-start(f32[4,8,4,1024]{3,1,2,0:T(8,128)} %copy.17) | copy-start | bytes 1572868
  354.0 453.9 %copy-start.3 = (bf16[32,32,32]{2,1,0:T(8,128)(2,1)S(1)}, bf16[32,32,32]{2,1,0:T(8,128)(2,1)}, u32[]{:S(2)}) copy-start(bf16[32,32,32]{2,1,0:T(8,128)(2,1)} %reshape.101) | copy-start | bytes 196612
  (49 other events, 1844.4 us)
Sparse Core Ops, SparseCore 0:
  10.7 205.4 all-gather.1
  361.2 165.3 reduce-scatter.3
